TPU v7x, 32 devices: a whole 2x2x4 slice. The times are simulated.
32 devices in a mesh: groups: 2 (over y), ctx: 4 (over z), head: 2 (over x), sub: 2 (over core).
Axes of the slice: x: 2, y: 2, z: 4, core: 2. Of those that a mesh axis runs over, the one named last changes fastest.
Arguments:
- queries: bfloat16 [2048, 64, 128], P(('groups', 'ctx', 'sub'), 'head'), parts along dimension 0, may hold values from -6 to 6
- keys: bfloat16 [2048, 4, 128], P(('groups', 'ctx', 'sub'), 'head'), parts along dimension 0, may hold values from -6 to 6
- values: bfloat16 [2048, 4, 128], P(('groups', 'ctx', 'sub'), 'head'), parts along dimension 0, may hold values from -6 to 6
- grad_out: bfloat16 [2048, 64, 128], P(('groups', 'ctx', 'sub'), 'head'), parts along dimension 0, may hold values from -9 to 9
- row_lse: float32 [2048, 64], P(('groups', 'ctx', 'sub'), 'head'), parts along dimension 0, may hold values from 5.5 to 6.5
- row_delta: float32 [2048, 64], P(('groups', 'ctx', 'sub'), 'head'), parts along dimension 0, may hold values from -24 to 24
- doc_ids: int32 [2048], P(('groups', 'ctx', 'sub')), parts along dimension 0, may hold values from 0 to 3, never falling along the last dimension, each value on 1 to 512 neighbouring positions
- pairs: int32 [16, 2], P('groups'), parts along dimension 0, may hold values from 0 to 7, as said below
Outputs:
- grad_queries: float32 [2048, 64, 128], P(('groups', 'ctx', 'sub'), 'head'), parts along dimension 0
- grad_keys: float32 [2048, 4, 128], P(('groups', 'ctx', 'sub'), 'head'), parts along dimension 0
- grad_values: float32 [2048, 4, 128], P(('groups', 'ctx', 'sub'), 'head'), parts along dimension 0
There are 2 independent parts, one for each index of `groups`. A program takes and returns all parts, laid end to end along the dimension named above; each array names one. Nothing has to cross between parts.
Inputs may be any that keep to these rules, and one draw needn't show every extreme that they name: `pairs`: row c holds two different span indices, neither equal to c. `doc_ids`: never falls along the tokens; every document appears.
All inputs are finite; a program needn't handle non-finite values.
Results may differ from a plain program's by a relative error of at most 0.0046.
Values may be sent and summed in bfloat16 or wider, within the bound.
A program may use at most 64 MiB of HBM per device.

v0:
```python
import functools
import math

import jax
import jax.numpy as jnp
from jax import lax
from jax.experimental import pallas as pl
from jax.experimental.pallas import tpu as pltpu
from jax.sharding import PartitionSpec as P

BF = jnp.bfloat16
F32 = jnp.float32
MESH = pl.DeviceIdType.MESH


def pieces_of(x):
    hi = x.astype(BF)
    rest = x - hi.astype(F32)
    mid = rest.astype(BF)
    lo = (rest - mid.astype(F32)).astype(BF)
    return hi, mid, lo


def kernel(
    dims,
    pairs_ref, docs_ref, lse_ref, delta_ref, keys_ref, vals_ref, q_hbm, up_hbm,
    dq_hbm, dk_ref, dv_ref,
    own_ref, q_vm, up_vm, qa, da, bias, kfar, vfar, kloc, vloc,
    dq_vm, dq_low, dk_loc, dv_loc, kv_all, send_a, recv_a, send_b, recv_b,
    in_sem, out_sem, z_send, p_send, z_recv, p_recv, a_send, a_recv, b_send, b_recv,
):
    zs, ss, rows, kvh, grp, hd, tile_tok = dims
    spans = zs * ss
    stripe = rows // spans
    factor = hd ** -0.5
    scale2 = factor * math.log2(math.e)
    z = lax.axis_index("ctx")
    s = lax.axis_index("sub")
    me = z * ss + s
    tiles = rows // tile_tok
    tr = tile_tok * grp

    ins = [
        pltpu.make_async_copy(q_hbm, q_vm, in_sem.at[0]),
        pltpu.make_async_copy(up_hbm, up_vm, in_sem.at[1]),
    ]
    for c in ins:
        c.start()

    barrier = pltpu.get_barrier_semaphore()

    def peer_of(off):
        d = lax.rem(me + off, spans)
        return d, d // ss, lax.rem(d, ss)

    def greet(dz, ds):
        pl.semaphore_signal(barrier, inc=1, device_id={"ctx": dz, "sub": ds}, device_id_type=MESH)

    greet(z, 1 - s)

    @pl.when(z > 0)
    def _():
        greet(z - 1, s)

    @pl.when(z < zs - 1)
    def _():
        greet(z + 1, s)


    pick_t = lax.broadcasted_iota(jnp.int32, (rows, rows * kvh), 0)
    pick_r = lax.broadcasted_iota(jnp.int32, (rows, rows * kvh), 1)
    for g in range(kvh):
        pick = jnp.where(pick_r == pick_t * kvh + g, 1.0, 0.0).astype(BF)
        for part, ref in enumerate((keys_ref, vals_ref)):
            took = jnp.dot(pick, ref[...], preferred_element_type=F32)
            own_ref[g, :, part * hd:(part + 1) * hd] = took.astype(BF)

    pos_t = lax.broadcasted_iota(jnp.int32, (rows, rows), 0)
    pos_u = lax.broadcasted_iota(jnp.int32, (rows, rows), 1)
    doc_u = jnp.broadcast_to(docs_ref[...].astype(F32), (rows, rows))
    doc_t = doc_u.T
    bias[...] = jnp.where((pos_t >= pos_u) & (doc_u == doc_t), 0.0, -3e38)

    heads = kvh * grp
    put_h = lax.broadcasted_iota(jnp.int32, (heads, hd), 0)
    put_l = lax.broadcasted_iota(jnp.int32, (heads, hd), 1)

    def lanes_of(x):
        total = jnp.zeros((rows, hd), F32)
        for i, piece in enumerate(pieces_of(x)):
            place = jnp.where(put_l == put_h + i * heads, 1.0, 0.0).astype(BF)
            total = total + lax.dot_general(
                piece, place, (((0,), (0,)), ((), ())), preferred_element_type=F32
            )
        return total.astype(BF)

    lse_l = lanes_of(lse_ref[...] * (hd ** 0.5))
    del_l = lanes_of(delta_ref[...])
    row_h = lax.broadcasted_iota(jnp.int32, (grp, hd), 0)
    row_l = lax.broadcasted_iota(jnp.int32, (grp, hd), 1)
    used = lax.broadcasted_iota(jnp.int32, (rows, hd), 1) < 3 * heads
    neg = jnp.where(used, -1.0, 0.0).astype(BF)

    ends = jnp.where(z > 0, 1, 0) + jnp.where(z < zs - 1, 1, 0)
    pl.semaphore_wait(barrier, 1 + ends)


    other = 1 - s

    def to_line(g, slot, src, dz, way):
        return pltpu.make_async_remote_copy(
            src_ref=src, dst_ref=kv_all[g].at[slot],
            send_sem=z_send.at[g, slot, way], recv_sem=z_recv.at[g, slot],
            device_id={"ctx": dz, "sub": s}, device_id_type=MESH)

    def to_partner(g, slot, src):
        return pltpu.make_async_remote_copy(
            src_ref=src, dst_ref=kv_all[g].at[slot],
            send_sem=p_send.at[g, slot], recv_sem=p_recv.at[g, slot],
            device_id={"ctx": z, "sub": other}, device_id_type=MESH)

    def spread(g, slot, src, do, right, left):
        @pl.when(right)
        def _():
            c = to_line(g, slot, src, z + 1, 0)
            c.start() if do else c.wait_send()

        @pl.when(left)
        def _():
            c = to_line(g, slot, src, z - 1, 1)
            c.start() if do else c.wait_send()

        c = to_partner(g, slot, src)
        c.start() if do else c.wait_send()

    def own_step(g, do):
        spread(g, me, own_ref.at[g], do, z < zs - 1, z > 0)

    def relay_step(g, j, do):
        @pl.when(z - j >= 0)
        def _():
            slot = (z - j) * ss + s
            if do:
                to_line(g, slot, own_ref.at[g], z, 0).wait_recv()
            spread(g, slot, kv_all[g].at[slot], do, z < zs - 1, z < 0)

        @pl.when(z + j < zs)
        def _():
            slot = (z + j) * ss + s
            if do:
                to_line(g, slot, own_ref.at[g], z, 0).wait_recv()
            spread(g, slot, kv_all[g].at[slot], do, z < 0, z > 0)

    def partner_wait(g):
        for a in range(zs):
            slot = a * ss + other
            to_partner(g, slot, own_ref.at[g]).wait_recv()

    for g in range(kvh):
        own_step(g, True)

    for c in ins:
        c.wait()

    def attend(g, qa, da, kcat, vcat, local):
        nk = kcat.shape[0]

        def step(i, carry):
            dk, dv = carry
            rs = pl.ds(pl.multiple_of(i * tr, tr), tr)
            ts = pl.ds(pl.multiple_of(i * tile_tok, tile_tok), tile_tok)
            qt = qa[rs, :]
            ut = da[rs, :]
            nt = (((1,), (1,)), ((), ()))
            x = lax.dot_general(qt, kcat[...], nt, preferred_element_type=F32)
            y = lax.dot_general(ut, vcat[...], nt, preferred_element_type=F32)
            if local:
                x = (x.reshape(tile_tok, grp, nk) + bias[ts, :][:, None, :]).reshape(tr, nk)
            p = jnp.exp2(x * scale2)
            ds_low = (p * y).astype(BF)
            p_low = p.astype(BF)
            dq = jnp.dot(ds_low, kcat[:, :hd], preferred_element_type=F32)
            tn = (((0,), (0,)), ((), ()))
            dk = dk + lax.dot_general(ds_low, qt[:, :hd], tn, preferred_element_type=F32)
            dv = dv + lax.dot_general(p_low, ut[:, :hd], tn, preferred_element_type=F32)
            sl = pl.ds(g * grp, grp)
            dq = dq.reshape(tile_tok, grp, hd)
            if local:
                dq_vm[ts, sl, :] = dq
            else:
                dq_low[ts, sl, :] = ((dq_vm[ts, sl, :] + dq) * factor).astype(BF)
            return dk, dv

        zero = jnp.zeros((nk, hd), F32)
        return lax.fori_loop(0, tiles, step, (zero, zero))

    def near(g):
        build_g(g)
        kloc[:, :hd] = own_ref[g, :, :hd]
        kloc[:, hd:] = neg
        vloc[:, :hd] = own_ref[g, :, hd:]
        vloc[:, hd:] = neg
        dk, dv = attend(g, qa.at[g], da.at[g], kloc, vloc, True)
        dk_loc[g] = dk
        dv_loc[g] = dv

    def build_g(g):
        head = row_h + g * grp
        hit = (row_l == head) | (row_l == head + heads) | (row_l == head + 2 * heads)
        keep = jnp.where(hit, 1.0, 0.0).astype(BF)
        sl = pl.ds(g * grp, grp)
        qa[g, :, :hd] = q_vm[:, sl, :].reshape(rows * grp, hd)
        da[g, :, :hd] = up_vm[:, sl, :].reshape(rows * grp, hd)
        qa[g, :, hd:] = (lse_l[:, None, :] * keep[None]).reshape(rows * grp, hd)
        da[g, :, hd:] = (del_l[:, None, :] * keep[None]).reshape(rows * grp, hd)

    def a_copy(g, off):
        d, dz, ds = peer_of(off)
        return pltpu.make_async_remote_copy(
            src_ref=send_a.at[g, d], dst_ref=recv_a.at[g, me],
            send_sem=a_send.at[g, off], recv_sem=a_recv.at[g, off],
            device_id={"ctx": dz, "sub": ds}, device_id_type=MESH)

    def b_copy(g, off):
        d, dz, ds = peer_of(off)
        return pltpu.make_async_remote_copy(
            src_ref=send_b.at[g, d], dst_ref=recv_b.at[g, me],
            send_sem=b_send.at[g, off], recv_sem=b_recv.at[g, off],
            device_id={"ctx": dz, "sub": ds}, device_id_type=MESH)

    def dq_copy(g):
        sl = pl.ds(g * grp, grp)
        return pltpu.make_async_copy(dq_low.at[:, sl, :], dq_hbm.at[:, sl, :], out_sem.at[g])

    def far(g):
        for j in range(2):
            blk = kv_all[g][pairs_ref[j, me]]
            js = pl.ds(j * rows, rows)
            kfar[js, :hd] = blk[:, :hd]
            kfar[js, hd:] = neg
            vfar[js, :hd] = blk[:, hd:]
            vfar[js, hd:] = neg
        dk, dv = attend(g, qa.at[g], da.at[g], kfar, vfar, False)
        for j in range(2):
            js = slice(j * rows, (j + 1) * rows)
            send_a[g, :, j, :, :hd] = dk[js].astype(BF).reshape(spans, stripe, hd)
            send_a[g, :, j, :, hd:] = dv[js].astype(BF).reshape(spans, stripe, hd)
        recv_a[g, me] = send_a[g, me]
        for off in range(1, spans):
            a_copy(g, off).start()
        dq_copy(g).start()

    def combine(g):
        for off in range(1, spans):
            a_copy(g, off).wait_recv()

        def owner(o, _):
            total = jnp.zeros((stripe, 2 * hd), F32)
            for src in range(spans):
                for j in range(2):
                    got = recv_a[g, src, j].astype(F32)
                    total = total + jnp.where(pairs_ref[j, src] == o, got, 0.0)
            send_b[g, o] = total.astype(BF)
            return 0

        lax.fori_loop(0, spans, owner, 0)
        recv_b[g, me] = send_b[g, me]
        for off in range(1, spans):
            b_copy(g, off).start()

    def finish(g):
        for off in range(1, spans):
            b_copy(g, off).wait_recv()
        home = recv_b[g].reshape(rows, 2 * hd).astype(F32)
        at = pl.ds(g, rows, stride=kvh)
        dk_ref[at, :] = (dk_loc[g] + home[:, :hd]) * factor
        dv_ref[at, :] = dv_loc[g] + home[:, hd:]

    for g in range(kvh):
        near(g)
        relay_step(g, 1, True)
        if g > 0 and zs > 2:
            relay_step(g - 1, 2, True)
    for g in range(kvh):
        first = 2 if g == kvh - 1 else 3
        for j in range(first, zs):
            relay_step(g, j, True)
    for g in range(kvh):
        own = own_ref[g]
        kv_all[g][me] = own
    for g in range(kvh):
        partner_wait(g)
        far(g)
    for g in range(kvh):
        combine(g)
    for g in range(kvh):
        finish(g)
    for g in range(kvh):
        dq_copy(g).wait()
        own_step(g, False)
        for j in range(1, zs):
            relay_step(g, j, False)
        for off in range(1, spans):
            a_copy(g, off).wait_send()
            b_copy(g, off).wait_send()


def tail_kernel(chunks, dq_in, dk_in, dv_in, dq_out, dk_out, dv_out, low, wide, dk_vm, dv_vm, in_sem, out_sem):
    size = low.shape[0] // chunks
    near = ((dk_in, dk_vm, dk_out), (dv_in, dv_vm, dv_out))
    reads = [
        pltpu.make_async_copy(
            dq_in.at[pl.ds(i * size, size)], low.at[pl.ds(i * size, size)], in_sem.at[i])
        for i in range(chunks)
    ]
    reads += [
        pltpu.make_async_copy(src, mid, in_sem.at[chunks + i])
        for i, (src, mid, _) in enumerate(near)
    ]
    for c in reads:
        c.start()
    writes = []
    for i in range(chunks):
        reads[i].wait()
        part = pl.ds(i * size, size)
        wide[part] = low[part].astype(F32)
        writes.append(pltpu.make_async_copy(wide.at[part], dq_out.at[part], out_sem.at[i]))
        writes[-1].start()
    for i, (_, mid, dst) in enumerate(near):
        reads[chunks + i].wait()
        writes.append(pltpu.make_async_copy(mid, dst, out_sem.at[chunks + i]))
        writes[-1].start()
    for c in writes:
        c.wait()


def widened(dq, dk, dv):
    hbm = pl.BlockSpec(memory_space=pltpu.HBM)
    chunks = 4
    return pl.pallas_call(
        functools.partial(tail_kernel, chunks),
        out_shape=tuple(jax.ShapeDtypeStruct(x.shape, F32) for x in (dq, dk, dv)),
        in_specs=[hbm] * 3,
        out_specs=(hbm,) * 3,
        scratch_shapes=[
            pltpu.VMEM(dq.shape, BF),
            pltpu.VMEM(dq.shape, F32),
            pltpu.VMEM(dk.shape, F32),
            pltpu.VMEM(dv.shape, F32),
            pltpu.SemaphoreType.DMA((chunks + 2,)),
            pltpu.SemaphoreType.DMA((chunks + 2,)),
        ],
        name="widen",
    )(dq, dk, dv)


def fused(zs, ss, queries, keys, values, grad_out, row_lse, row_delta, doc_ids, pairs):
    rows, qh, hd = queries.shape
    kvh = keys.shape[1]
    grp = qh // kvh
    spans = zs * ss
    stripe = rows // spans
    tile_tok = 128
    vm = pl.BlockSpec(memory_space=pltpu.VMEM)
    sm = pl.BlockSpec(memory_space=pltpu.SMEM)
    hbm = pl.BlockSpec(memory_space=pltpu.HBM)
    dma = pltpu.SemaphoreType.DMA
    dq, dk, dv = pl.pallas_call(
        functools.partial(kernel, (zs, ss, rows, kvh, grp, hd, tile_tok)),
        out_shape=(
            jax.ShapeDtypeStruct((rows, qh, hd), BF),
            jax.ShapeDtypeStruct((rows * kvh, hd), F32),
            jax.ShapeDtypeStruct((rows * kvh, hd), F32),
        ),
        in_specs=[sm, vm, vm, vm, vm, vm, hbm, hbm],
        out_specs=(pl.BlockSpec(memory_space=pl.ANY), vm, vm),
        scratch_shapes=[
            pltpu.VMEM((kvh, rows, 2 * hd), BF),
            pltpu.VMEM((rows, qh, hd), BF),
            pltpu.VMEM((rows, qh, hd), BF),
            pltpu.VMEM((kvh, rows * grp, 2 * hd), BF),
            pltpu.VMEM((kvh, rows * grp, 2 * hd), BF),
            pltpu.VMEM((rows, rows), F32),
            pltpu.VMEM((2 * rows, 2 * hd), BF),
            pltpu.VMEM((2 * rows, 2 * hd), BF),
            pltpu.VMEM((rows, 2 * hd), BF),
            pltpu.VMEM((rows, 2 * hd), BF),
            pltpu.VMEM((rows, qh, hd), F32),
            pltpu.VMEM((rows, qh, hd), BF),
            pltpu.VMEM((kvh, rows, hd), F32),
            pltpu.VMEM((kvh, rows, hd), F32),
            [pltpu.VMEM((spans, rows, 2 * hd), BF) for _ in range(kvh)],
            pltpu.VMEM((kvh, spans, 2, stripe, 2 * hd), BF),
            pltpu.VMEM((kvh, spans, 2, stripe, 2 * hd), BF),
            pltpu.VMEM((kvh, spans, stripe, 2 * hd), BF),
            pltpu.VMEM((kvh, spans, stripe, 2 * hd), BF),
            dma((2,)),
            dma((kvh,)),
            dma((kvh, spans, 2)),
            dma((kvh, spans)),
            dma((kvh, spans)),
            dma((kvh, spans)),
            dma((kvh, spans)),
            dma((kvh, spans)),
            dma((kvh, spans)),
            dma((kvh, spans)),
        ],
        compiler_params=pltpu.CompilerParams(collective_id=0, has_side_effects=True),
        name="span_grads",
    )(
        pairs.T, doc_ids.reshape(1, rows), row_lse.T, row_delta.T,
        keys.reshape(rows * kvh, hd), values.reshape(rows * kvh, hd), queries, grad_out,
    )
    dq, dk, dv = widened(dq, dk, dv)
    return dq, dk.reshape(rows, kvh, hd), dv.reshape(rows, kvh, hd)


QH = 64
KVH = 4


def block_terms(query_blk, upstream, log_norm, row_terms, key_blk, value_blk, allowed, factor):
    scores = (
        jnp.einsum("tghd,kgd->tghk", query_blk, key_blk, preferred_element_type=jnp.float32)
        * factor
    )
    probs = jnp.exp(scores - log_norm[..., None])
    if allowed is not None:
        probs = jnp.where(allowed[:, None, None, :], probs, 0.0)
    grad_probs = jnp.einsum(
        "tghd,kgd->tghk", upstream, value_blk, preferred_element_type=jnp.float32
    )
    grad_scores = probs * (grad_probs - row_terms[..., None])
    probs_low = probs.astype(jnp.bfloat16)
    scores_low = grad_scores.astype(jnp.bfloat16)
    grad_val = jnp.einsum("tghk,tghd->kgd", probs_low, upstream, preferred_element_type=jnp.float32)
    grad_key = (
        jnp.einsum("tghk,tghd->kgd", scores_low, query_blk, preferred_element_type=jnp.float32)
        * factor
    )
    grad_query = (
        jnp.einsum("tghk,kgd->tghd", scores_low, key_blk, preferred_element_type=jnp.float32)
        * factor
    )
    return (grad_query, grad_key, grad_val)


def body(zs, ss, queries, keys, values, grad_out, row_lse, row_delta, doc_ids, pairs):
    grp = queries.shape[1] // keys.shape[1]
    if (
        ss == 2
        and queries.shape[0] % (16 * zs * ss) == 0
        and grp % 16 == 0
        and 3 * queries.shape[1] <= queries.shape[2]
    ):
        return fused(
            zs, ss, queries, keys, values, grad_out, row_lse, row_delta, doc_ids, pairs
        )
    rows_here = queries.shape[0]
    heads_here = keys.shape[1]
    head_dim = keys.shape[2]
    grouped = QH // KVH
    factor = head_dim ** (-0.5)
    spans = lax.axis_size(("ctx", "sub"))
    stripe = rows_here // spans
    query_blk = queries.reshape(rows_here, heads_here, grouped, head_dim)
    upstream = grad_out.reshape(rows_here, heads_here, grouped, head_dim)
    log_norm = row_lse.reshape(rows_here, heads_here, grouped)
    row_terms = row_delta.reshape(rows_here, heads_here, grouped)
    positions = jnp.arange(rows_here, dtype=jnp.int32)
    allowed = (positions[:, None] >= positions[None, :]) & (doc_ids[:, None] == doc_ids[None, :])
    query_sum, key_local, value_local = block_terms(
        query_blk, upstream, log_norm, row_terms, keys, values, allowed, factor
    )
    stacked = jnp.concatenate([keys, values], axis=2).reshape(rows_here, heads_here * 2 * head_dim)
    features = stacked.shape[1]
    spread = lax.all_to_all(
        stacked.reshape(spans, stripe, features),
        ("ctx", "sub"),
        split_axis=0,
        concat_axis=0,
        tiled=True,
    )
    wanted = jnp.take(spread, pairs.T, axis=0)
    remote = lax.all_to_all(
        wanted, ("ctx", "sub"), split_axis=1, concat_axis=1, tiled=True
    ).reshape(2, rows_here, features)
    remote = remote.reshape(2, rows_here, heads_here, 2 * head_dim)
    returned = []
    for which in range(2):
        far_keys = remote[which, :, :, :head_dim]
        far_values = remote[which, :, :, head_dim:]
        query_part, key_part, value_part = block_terms(
            query_blk, upstream, log_norm, row_terms, far_keys, far_values, None, factor
        )
        query_sum = query_sum + query_part
        returned.append(
            jnp.concatenate([key_part, value_part], axis=2).reshape(rows_here, features)
        )
    outgoing = jnp.stack(returned).reshape(2, spans, stripe, features)
    incoming = lax.all_to_all(outgoing, ("ctx", "sub"), split_axis=1, concat_axis=1, tiled=True)
    owners = pairs.T.reshape(-1)
    select = (jnp.arange(spans, dtype=jnp.int32)[:, None] == owners[None, :]).astype(jnp.float32)
    summed = jnp.dot(
        select,
        incoming.reshape(2 * spans, stripe * features),
        precision=lax.Precision.HIGHEST,
        preferred_element_type=jnp.float32,
    )
    at_home = lax.all_to_all(
        summed.reshape(spans, stripe, features),
        ("ctx", "sub"),
        split_axis=0,
        concat_axis=0,
        tiled=True,
    )
    at_home = at_home.reshape(rows_here, heads_here, 2 * head_dim)
    grad_keys = key_local + at_home[:, :, :head_dim]
    grad_values = value_local + at_home[:, :, head_dim:]
    grad_queries = query_sum.reshape(rows_here, heads_here * grouped, head_dim)
    return (grad_queries, grad_keys, grad_values)


def solution(mesh):
    return jax.shard_map(
        functools.partial(body, mesh.shape["ctx"], mesh.shape["sub"]),
        mesh=mesh,
        in_specs=(
            P(("groups", "ctx", "sub"), "head", None),
            P(("groups", "ctx", "sub"), "head", None),
            P(("groups", "ctx", "sub"), "head", None),
            P(("groups", "ctx", "sub"), "head", None),
            P(("groups", "ctx", "sub"), "head"),
            P(("groups", "ctx", "sub"), "head"),
            P(("groups", "ctx", "sub")),
            P("groups", None),
        ),
        out_specs=(
            P(("groups", "ctx", "sub"), "head", None),
            P(("groups", "ctx", "sub"), "head", None),
            P(("groups", "ctx", "sub"), "head", None),
        ),
        check_vma=False,
    )
```

profile of v0, /device:TPU:0, one launch (start us, length us, event | category | flops | bytes accessed | tf_op | source)
XLA Modules:
  0.0 34.1 jit_solution(17652646737879707084)
XLA Ops:
  0.6 31.0 %span_grads.1 = (bf16[128,32,128]{2,1,0:T(8,128)(2,1)}, f32[256,128]{1,0:T(8,128)}, f32[256,128]{1,0:T(8,128)}) custom-call(s32[2,8]{1,0:T(2,128)} %bitcast.12, s32[1,128]{1,0:T(1,128)} %bitcast.13, f32[32,128]{1,0:T(8,128)} %bitcast.10, f32[32,128]{1,0:T(8,128)} %bitcast.11, bf16[256,128]{1,0:T(8,128)(2,1)} %bitcast.8, bf16[256,128]{1,0:T(8,128)(2,1)} %bitcast.9, ...), custom_call_target="tpu_custom_call" | custom-call | tf_op jit(solution)/shard_map/span_grads/pallas_call | solution.py:368
  31.6 2.5 %widen.1 = (f32[128,32,128]{2,1,0:T(8,128)}, f32[256,128]{1,0:T(8,128)}, f32[256,128]{1,0:T(8,128)}) custom-call(bf16[128,32,128]{2,1,0:T(8,128)(2,1)} %get-tuple-element.9.dq_in, f32[256,128]{1,0:T(8,128)} %get-tuple-element.10.dk_in, f32[256,128]{1,0:T(8,128)} %get-tuple-element.11.dv_in), custom_call_target="tpu_custom_call" | custom-call | tf_op jit(solution)/shard_map/widen/pallas_call | solution.py:340
where the time goes:
time: 34.3 us; the launch traced here: 34.1 us
  Pallas kernels  33.5 us (98%)
  between operations  0.64 us (2%)
    pallas_call x1, Pallas kernels, fused(): pl.pallas_call(functools.partial(kernel, (zs, ss, rows, kvh, grp, hd, til...  31 us
    pallas_call x1, Pallas kernels, widened(): pl.pallas_call(functools.partial(tail_kernel, chunks), out_shape=tuple((j...  2.48 us

commit v1 on v0

--- a/solution.py
+++ b/solution.py
@@ -24,10 +24,10 @@
 def kernel(
     dims,
     pairs_ref, docs_ref, lse_ref, delta_ref, keys_ref, vals_ref, q_hbm, up_hbm,
-    dq_hbm, dk_ref, dv_ref,
+    dq_vm, dk_ref, dv_ref,
     own_ref, q_vm, up_vm, qa, da, bias, kfar, vfar, kloc, vloc,
-    dq_vm, dq_low, dk_loc, dv_loc, kv_all, send_a, recv_a, send_b, recv_b,
-    in_sem, out_sem, z_send, p_send, z_recv, p_recv, a_send, a_recv, b_send, b_recv,
+    dk_loc, dv_loc, kv_all, send_a, recv_a, send_b, recv_b,
+    in_sem, z_send, p_send, z_recv, p_recv, a_send, a_recv, b_send, b_recv,
 ):
     zs, ss, rows, kvh, grp, hd, tile_tok = dims
     spans = zs * ss
@@ -188,7 +188,7 @@
             if local:
                 dq_vm[ts, sl, :] = dq
             else:
-                dq_low[ts, sl, :] = ((dq_vm[ts, sl, :] + dq) * factor).astype(BF)
+                dq_vm[ts, sl, :] = (dq_vm[ts, sl, :] + dq) * factor
             return dk, dv
 
         zero = jnp.zeros((nk, hd), F32)
@@ -227,10 +227,6 @@
             src_ref=send_b.at[g, d], dst_ref=recv_b.at[g, me],
             send_sem=b_send.at[g, off], recv_sem=b_recv.at[g, off],
             device_id={"ctx": dz, "sub": ds}, device_id_type=MESH)
-
-    def dq_copy(g):
-        sl = pl.ds(g * grp, grp)
-        return pltpu.make_async_copy(dq_low.at[:, sl, :], dq_hbm.at[:, sl, :], out_sem.at[g])
 
     def far(g):
         for j in range(2):
@@ -248,7 +244,6 @@
         recv_a[g, me] = send_a[g, me]
         for off in range(1, spans):
             a_copy(g, off).start()
-        dq_copy(g).start()
 
     def combine(g):
         for off in range(1, spans):
@@ -296,7 +291,6 @@
     for g in range(kvh):
         finish(g)
     for g in range(kvh):
-        dq_copy(g).wait()
         own_step(g, False)
         for j in range(1, zs):
             relay_step(g, j, False)
@@ -305,52 +299,26 @@
             b_copy(g, off).wait_send()
 
 
-def tail_kernel(chunks, dq_in, dk_in, dv_in, dq_out, dk_out, dv_out, low, wide, dk_vm, dv_vm, in_sem, out_sem):
-    size = low.shape[0] // chunks
-    near = ((dk_in, dk_vm, dk_out), (dv_in, dv_vm, dv_out))
-    reads = [
-        pltpu.make_async_copy(
-            dq_in.at[pl.ds(i * size, size)], low.at[pl.ds(i * size, size)], in_sem.at[i])
-        for i in range(chunks)
+def tail_kernel(dq_vm, dk_vm, dv_vm, dq_out, dk_out, dv_out, sems):
+    copies = [
+        pltpu.make_async_copy(src, dst, sems.at[i])
+        for i, (src, dst) in enumerate(((dq_vm, dq_out), (dk_vm, dk_out), (dv_vm, dv_out)))
     ]
-    reads += [
-        pltpu.make_async_copy(src, mid, in_sem.at[chunks + i])
-        for i, (src, mid, _) in enumerate(near)
-    ]
-    for c in reads:
+    for c in copies:
         c.start()
-    writes = []
-    for i in range(chunks):
-        reads[i].wait()
-        part = pl.ds(i * size, size)
-        wide[part] = low[part].astype(F32)
-        writes.append(pltpu.make_async_copy(wide.at[part], dq_out.at[part], out_sem.at[i]))
-        writes[-1].start()
-    for i, (_, mid, dst) in enumerate(near):
-        reads[chunks + i].wait()
-        writes.append(pltpu.make_async_copy(mid, dst, out_sem.at[chunks + i]))
-        writes[-1].start()
-    for c in writes:
+    for c in copies:
         c.wait()
 
 
-def widened(dq, dk, dv):
-    hbm = pl.BlockSpec(memory_space=pltpu.HBM)
-    chunks = 4
+def written(dq, dk, dv):
     return pl.pallas_call(
-        functools.partial(tail_kernel, chunks),
+        tail_kernel,
         out_shape=tuple(jax.ShapeDtypeStruct(x.shape, F32) for x in (dq, dk, dv)),
-        in_specs=[hbm] * 3,
-        out_specs=(hbm,) * 3,
-        scratch_shapes=[
-            pltpu.VMEM(dq.shape, BF),
-            pltpu.VMEM(dq.shape, F32),
-            pltpu.VMEM(dk.shape, F32),
-            pltpu.VMEM(dv.shape, F32),
-            pltpu.SemaphoreType.DMA((chunks + 2,)),
-            pltpu.SemaphoreType.DMA((chunks + 2,)),
-        ],
-        name="widen",
+        in_specs=[pl.BlockSpec(memory_space=pltpu.VMEM)] * 3,
+        out_specs=(pl.BlockSpec(memory_space=pltpu.HBM),) * 3,
+        scratch_shapes=[pltpu.SemaphoreType.DMA((3,))],
+        compiler_params=pltpu.CompilerParams(vmem_limit_bytes=4 * 1024 * 1024),
+        name="write_out",
     )(dq, dk, dv)
 
 
@@ -368,12 +336,12 @@
     dq, dk, dv = pl.pallas_call(
         functools.partial(kernel, (zs, ss, rows, kvh, grp, hd, tile_tok)),
         out_shape=(
-            jax.ShapeDtypeStruct((rows, qh, hd), BF),
-            jax.ShapeDtypeStruct((rows * kvh, hd), F32),
-            jax.ShapeDtypeStruct((rows * kvh, hd), F32),
+            pltpu.VMEM((rows, qh, hd), F32),
+            pltpu.VMEM((rows * kvh, hd), F32),
+            pltpu.VMEM((rows * kvh, hd), F32),
         ),
         in_specs=[sm, vm, vm, vm, vm, vm, hbm, hbm],
-        out_specs=(pl.BlockSpec(memory_space=pl.ANY), vm, vm),
+        out_specs=(vm, vm, vm),
         scratch_shapes=[
             pltpu.VMEM((kvh, rows, 2 * hd), BF),
             pltpu.VMEM((rows, qh, hd), BF),
@@ -385,8 +353,6 @@
             pltpu.VMEM((2 * rows, 2 * hd), BF),
             pltpu.VMEM((rows, 2 * hd), BF),
             pltpu.VMEM((rows, 2 * hd), BF),
-            pltpu.VMEM((rows, qh, hd), F32),
-            pltpu.VMEM((rows, qh, hd), BF),
             pltpu.VMEM((kvh, rows, hd), F32),
             pltpu.VMEM((kvh, rows, hd), F32),
             [pltpu.VMEM((spans, rows, 2 * hd), BF) for _ in range(kvh)],
@@ -395,7 +361,6 @@
             pltpu.VMEM((kvh, spans, stripe, 2 * hd), BF),
             pltpu.VMEM((kvh, spans, stripe, 2 * hd), BF),
             dma((2,)),
-            dma((kvh,)),
             dma((kvh, spans, 2)),
             dma((kvh, spans)),
             dma((kvh, spans)),
@@ -411,7 +376,7 @@
         pairs.T, doc_ids.reshape(1, rows), row_lse.T, row_delta.T,
         keys.reshape(rows * kvh, hd), values.reshape(rows * kvh, hd), queries, grad_out,
     )
-    dq, dk, dv = widened(dq, dk, dv)
+    dq, dk, dv = written(dq, dk, dv)
     return dq, dk.reshape(rows, kvh, hd), dv.reshape(rows, kvh, hd)
 
 

time: 34.3 us -> 32.6 us (0.950)
  Pallas kernels: 33.5 us -> 31.7 us
    pallas_call x1, Pallas kernels: 2.48 us -> 1.42 us  [written(): pl.pallas_call(tail_kernel, out_shape=tuple((jax.ShapeDtypeStruct(x.shape...]
    pallas_call x1, Pallas kernels: 31 us -> 30.3 us  [fused(): pl.pallas_call(functools.partial(kernel, (zs, ss, rows, kvh, grp, hd, til...]
where the time goes in v1:
time: 32.6 us; the launch traced here: 32.4 us
  Pallas kernels  31.7 us (97%)
  between operations  0.64 us (2%)
    pallas_call x1, Pallas kernels, fused(): pl.pallas_call(functools.partial(kernel, (zs, ss, rows, kvh, grp, hd, til...  30.3 us
    pallas_call x1, Pallas kernels, written(): pl.pallas_call(tail_kernel, out_shape=tuple((jax.ShapeDtypeStruct(x.shape...  1.42 us

profile of v1, /device:TPU:0, one launch (start us, length us, event | category | flops | bytes accessed | tf_op | source)
XLA Modules:
  0.0 32.4 jit_solution(11835403247586515177)
XLA Ops:
  0.6 30.3 %span_grads.1 = (f32[128,32,128]{2,1,0:T(8,128)S(1)}, f32[256,128]{1,0:T(8,128)S(1)}, f32[256,128]{1,0:T(8,128)S(1)}) custom-call(s32[2,8]{1,0:T(2,128)} %bitcast.12, s32[1,128]{1,0:T(1,128)} %bitcast.13, f32[32,128]{1,0:T(8,128)} %bitcast.10, f32[32,128]{1,0:T(8,128)} %bitcast.11, bf16[256,128]{1,0:T(8,128)(2,1)} %bitcast.8, bf16[256,128]{1,0:T(8,128)(2,1)} %bitcast.9, ...), custom_call_target="tpu_custom_call" | custom-call | tf_op jit(solution)/shard_map/span_grads/pallas_call | solution.py:336
  31.0 1.4 %write_out.1 = (f32[128,32,128]{2,1,0:T(8,128)}, f32[256,128]{1,0:T(8,128)}, f32[256,128]{1,0:T(8,128)}) custom-call(f32[128,32,128]{2,1,0:T(8,128)S(1)} %get-tuple-element.9.dq_vm, f32[256,128]{1,0:T(8,128)S(1)} %get-tuple-element.10.dk_vm, f32[256,128]{1,0:T(8,128)S(1)} %get-tuple-element.11.dv_vm), custom_call_target="tpu_custom_call" | custom-call | tf_op jit(solution)/shard_map/write_out/pallas_call | solution.py:314

commit v2 on v1

v2 whole, which is shorter than its diff:
```python
import functools
import math

import jax
import jax.numpy as jnp
from jax import lax
from jax.experimental import pallas as pl
from jax.experimental.pallas import tpu as pltpu
from jax.sharding import PartitionSpec as P

BF = jnp.bfloat16
F32 = jnp.float32
MESH = pl.DeviceIdType.MESH


def pieces_of(x):
    hi = x.astype(BF)
    rest = x - hi.astype(F32)
    mid = rest.astype(BF)
    lo = (rest - mid.astype(F32)).astype(BF)
    return hi, mid, lo


def kernel(
    dims,
    pairs_ref, docs_hbm, lse_hbm, delta_hbm, keys_hbm, vals_hbm, q_hbm, up_hbm,
    dq_vm, dk_ref, dv_ref,
    docs_ref, lse_ref, delta_ref, keys_ref, vals_ref, q_vm, up_vm,
    qa, da, bias, kfar, vfar, kloc, vloc, probs,
    dk_loc, dv_loc, kv, send_a, recv_a, send_b, recv_b,
    in_sem, z_send, p_send, z_recv, p_recv, a_send, a_recv, b_send, b_recv,
):
    zs, ss, rows, kvh, grp, hd = dims
    spans = zs * ss
    stripe = rows // spans
    chunks = 2 * kvh
    factor = hd ** -0.5
    scale2 = factor * math.log2(math.e)
    z = lax.axis_index("ctx")
    s = lax.axis_index("sub")
    me = z * ss + s
    other = 1 - s
    mine = s * zs + z
    nt = (((1,), (1,)), ((), ()))
    tn = (((0,), (0,)), ((), ()))

    barrier = pltpu.get_barrier_semaphore()

    def greet(dz, ds):
        pl.semaphore_signal(barrier, inc=1, device_id={"ctx": dz, "sub": ds}, device_id_type=MESH)

    greet(z, other)

    @pl.when(z > 0)
    def _():
        greet(z - 1, s)

    @pl.when(z < zs - 1)
    def _():
        greet(z + 1, s)

    ins = [
        pltpu.make_async_copy(src, dst, in_sem.at[i])
        for i, (src, dst) in enumerate((
            (keys_hbm, keys_ref), (vals_hbm, vals_ref), (lse_hbm, lse_ref), (delta_hbm, delta_ref),
            (docs_hbm, docs_ref), (q_hbm, q_vm), (up_hbm, up_vm),
        ))
    ]
    for c in ins:
        c.start()

    pick_t = lax.broadcasted_iota(jnp.int32, (rows, rows * kvh), 0)
    pick_r = lax.broadcasted_iota(jnp.int32, (rows, rows * kvh), 1)
    for part, ref in enumerate((keys_ref, vals_ref)):
        ins[part].wait()
        for g in range(kvh):
            pick = jnp.where(pick_r == pick_t * kvh + g, 1.0, 0.0).astype(BF)
            took = jnp.dot(pick, ref[...], preferred_element_type=F32)
            kv[g * 2 + part][mine] = took.astype(BF)

    ends = jnp.where(z > 0, 1, 0) + jnp.where(z < zs - 1, 1, 0)
    pl.semaphore_wait(barrier, 1 + ends)

    def to_line(c, slot, from_z, dz, way):
        return pltpu.make_async_remote_copy(
            src_ref=kv[c].at[slot], dst_ref=kv[c].at[slot],
            send_sem=z_send.at[c, way], recv_sem=z_recv.at[c, from_z],
            device_id={"ctx": dz, "sub": s}, device_id_type=MESH)

    def to_partner(c, slots):
        return pltpu.make_async_remote_copy(
            src_ref=kv[c].at[slots], dst_ref=kv[c].at[slots],
            send_sem=p_send.at[c], recv_sem=p_recv.at[c],
            device_id={"ctx": z, "sub": other}, device_id_type=MESH)

    def own_step(c):
        @pl.when(z < zs - 1)
        def _():
            to_line(c, mine, z, z + 1, 0).start()

        @pl.when(z > 0)
        def _():
            to_line(c, mine, z, z - 1, 1).start()

        to_partner(c, mine).start()

    def relay_step(c, j):
        @pl.when(z >= j)
        def _():
            slot = mine - j
            to_line(c, slot, z - j, z, 0).wait_recv()

            @pl.when(z < zs - 1)
            def _():
                to_line(c, slot, z - j, z + 1, 0).start()

            to_partner(c, slot).start()

        @pl.when(z + j < zs)
        def _():
            slot = mine + j
            to_line(c, slot, z + j, z, 1).wait_recv()

            @pl.when(z > 0)
            def _():
                to_line(c, slot, z + j, z - 1, 1).start()

            to_partner(c, slot).start()

    def line_sent(c):
        for at in range(zs):
            @pl.when(z == at)
            def _():
                if at < zs - 1:
                    to_line(c, pl.ds(0, at + 1), at, z, 0).wait_send()
                if at > 0:
                    to_line(c, pl.ds(0, zs - at), at, z, 1).wait_send()

        to_partner(c, pl.ds(0, zs)).wait_send()

    for c in range(chunks):
        own_step(c)

    for c in ins[2:5]:
        c.wait()
    pos_t = lax.broadcasted_iota(jnp.int32, (rows, rows), 0)
    pos_u = lax.broadcasted_iota(jnp.int32, (rows, rows), 1)
    doc_u = jnp.broadcast_to(docs_ref[...].astype(F32), (rows, rows))
    doc_t = doc_u.T
    bias[...] = jnp.where((pos_t >= pos_u) & (doc_u == doc_t), 0.0, -3e38)

    heads = kvh * grp
    put_h = lax.broadcasted_iota(jnp.int32, (heads, hd), 0)
    put_l = lax.broadcasted_iota(jnp.int32, (heads, hd), 1)

    def lanes_of(x):
        total = jnp.zeros((rows, hd), F32)
        for i, piece in enumerate(pieces_of(x)):
            place = jnp.where(put_l == put_h + i * heads, 1.0, 0.0).astype(BF)
            total = total + lax.dot_general(piece, place, tn, preferred_element_type=F32)
        return total.astype(BF)

    lse_l = lanes_of(lse_ref[...] * (hd ** 0.5))
    del_l = lanes_of(delta_ref[...])
    row_h = lax.broadcasted_iota(jnp.int32, (grp, hd), 0)
    row_l = lax.broadcasted_iota(jnp.int32, (grp, hd), 1)
    used = lax.broadcasted_iota(jnp.int32, (rows, hd), 1) < 3 * heads
    neg = jnp.where(used, -1.0, 0.0).astype(BF)
    kloc[:, hd:] = neg
    vloc[:, hd:] = neg
    for j in range(2):
        js = slice(j * rows, (j + 1) * rows)
        kfar[js, hd:] = neg
        vfar[js, hd:] = neg
    for c in ins[5:]:
        c.wait()

    def near(g):
        head = row_h + g * grp
        hit = (row_l == head) | (row_l == head + heads) | (row_l == head + 2 * heads)
        keep = jnp.where(hit, 1.0, 0.0).astype(BF)
        sl = pl.ds(g * grp, grp)
        qa[g, :, :hd] = q_vm[:, sl, :].reshape(rows * grp, hd)
        da[g, :, :hd] = up_vm[:, sl, :].reshape(rows * grp, hd)
        qa[g, :, hd:] = (lse_l[:, None, :] * keep[None]).reshape(rows * grp, hd)
        da[g, :, hd:] = (del_l[:, None, :] * keep[None]).reshape(rows * grp, hd)
        kloc[:, :hd] = kv[g * 2][mine]
        vloc[:, :hd] = kv[g * 2 + 1][mine]
        x = lax.dot_general(qa[g], kloc[...], nt, preferred_element_type=F32)
        y = lax.dot_general(da[g], vloc[...], nt, preferred_element_type=F32)
        x = (x.reshape(rows, grp, rows) + bias[...][:, None, :]).reshape(rows * grp, rows)
        p = jnp.exp2(x * scale2)
        ds_low = (p * y).astype(BF)
        p_low = p.astype(BF)
        dq = jnp.dot(ds_low, kloc[:, :hd], preferred_element_type=F32)
        dk_loc[g] = lax.dot_general(ds_low, qa[g, :, :hd], tn, preferred_element_type=F32)
        dv_loc[g] = lax.dot_general(p_low, da[g, :, :hd], tn, preferred_element_type=F32)
        dq_vm[:, sl, :] = dq.reshape(rows, grp, hd)

    def listed(c, dst):
        for j in range(2):
            span = pairs_ref[j, me]
            dst[pl.ds(j * rows, rows), :hd] = kv[c][lax.rem(span, ss) * zs + lax.div(span, ss)]

    def peer_of(off):
        d = lax.rem(me + off, spans)
        return d, {"ctx": d // ss, "sub": lax.rem(d, ss)}

    def give(c, total):
        for j in range(2):
            part = total[j * rows:(j + 1) * rows].astype(BF)
            send_a[c * spans:(c + 1) * spans, j] = part.reshape(spans, stripe, hd)
        recv_a[c * spans + me] = send_a[c * spans + me]
        for off in range(1, spans):
            d, at = peer_of(off)
            pltpu.make_async_remote_copy(
                src_ref=send_a.at[c * spans + d], dst_ref=recv_a.at[c * spans + me],
                send_sem=a_send.at[0], recv_sem=a_recv.at[c],
                device_id=at, device_id_type=MESH).start()

    def far_keys(g):
        listed(g * 2, kfar)
        x = lax.dot_general(qa[g], kfar[...], nt, preferred_element_type=F32)
        p = jnp.exp2(x * scale2)
        probs[...] = p
        give(g * 2 + 1, lax.dot_general(p.astype(BF), da[g, :, :hd], tn, preferred_element_type=F32))

    def far_vals(g):
        listed(g * 2 + 1, vfar)
        y = lax.dot_general(da[g], vfar[...], nt, preferred_element_type=F32)
        ds_low = (probs[...] * y).astype(BF)
        give(g * 2, lax.dot_general(ds_low, qa[g, :, :hd], tn, preferred_element_type=F32))
        dq = jnp.dot(ds_low, kfar[:, :hd], preferred_element_type=F32).reshape(rows, grp, hd)
        sl = pl.ds(g * grp, grp)
        dq_vm[:, sl, :] = (dq_vm[:, sl, :] + dq) * factor

    def many(ref, first, count, send_sem, recv_sem):
        return pltpu.make_async_remote_copy(
            src_ref=ref.at[pl.ds(first, count)], dst_ref=ref.at[pl.ds(first, count)],
            send_sem=send_sem, recv_sem=recv_sem,
            device_id={"ctx": z, "sub": other}, device_id_type=MESH)

    def combine(c):
        many(recv_a, c * spans, spans - 1, a_send.at[0], a_recv.at[c]).wait_recv()

        def owner(o, _):
            total = jnp.zeros((stripe, hd), F32)
            for src in range(spans):
                for j in range(2):
                    got = recv_a[c * spans + src, j].astype(F32)
                    total = total + jnp.where(pairs_ref[j, src] == o, got, 0.0)
            send_b[c * spans + o] = total.astype(BF)
            return 0

        lax.fori_loop(0, spans, owner, 0)
        recv_b[c * spans + me] = send_b[c * spans + me]
        for off in range(1, spans):
            d, at = peer_of(off)
            pltpu.make_async_remote_copy(
                src_ref=send_b.at[c * spans + d], dst_ref=recv_b.at[c * spans + me],
                send_sem=b_send.at[0], recv_sem=b_recv.at[c],
                device_id=at, device_id_type=MESH).start()

    def finish(c):
        g, part = c // 2, c % 2
        many(recv_b, c * spans, spans - 1, b_send.at[0], b_recv.at[c]).wait_recv()
        home = recv_b[c * spans:(c + 1) * spans].reshape(rows, hd).astype(F32)
        at = pl.ds(g, rows, stride=kvh)
        if part == 0:
            dk_ref[at, :] = (dk_loc[g] + home) * factor
        else:
            dv_ref[at, :] = dv_loc[g] + home

    def partner_wait(c):
        to_partner(c, pl.ds(other * zs, zs)).wait_recv()

    for g in range(kvh):
        near(g)
        relay_step(g * 2, 1)
        relay_step(g * 2 + 1, 1)
    for j in range(2, zs - 1):
        for c in range(chunks):
            relay_step(c, j)

    last = zs - 1
    if last > 1:
        relay_step(0, last)
        relay_step(1, last)
    for c in range(chunks):
        partner_wait(c)
        (far_keys if c % 2 == 0 else far_vals)(c // 2)
        if last > 1 and c + 2 < chunks:
            relay_step(c + 2, last)
    order = [g * 2 + part for g in range(kvh) for part in (1, 0)]
    for c in order:
        combine(c)
    for c in order:
        finish(c)
    for c in range(chunks):
        line_sent(c)
    many(send_a, 0, chunks * (spans - 1), a_send.at[0], a_recv.at[0]).wait_send()
    many(send_b, 0, chunks * (spans - 1), b_send.at[0], b_recv.at[0]).wait_send()


def tail_kernel(dq_vm, dk_vm, dv_vm, dq_out, dk_out, dv_out, sems):
    copies = [
        pltpu.make_async_copy(src, dst, sems.at[i])
        for i, (src, dst) in enumerate(((dq_vm, dq_out), (dk_vm, dk_out), (dv_vm, dv_out)))
    ]
    for c in copies:
        c.start()
    for c in copies:
        c.wait()


def written(dq, dk, dv):
    return pl.pallas_call(
        tail_kernel,
        out_shape=tuple(jax.ShapeDtypeStruct(x.shape, F32) for x in (dq, dk, dv)),
        in_specs=[pl.BlockSpec(memory_space=pltpu.VMEM)] * 3,
        out_specs=(pl.BlockSpec(memory_space=pltpu.HBM),) * 3,
        scratch_shapes=[pltpu.SemaphoreType.DMA((3,))],
        compiler_params=pltpu.CompilerParams(vmem_limit_bytes=4 * 1024 * 1024),
        name="write_out",
    )(dq, dk, dv)


def fused(zs, ss, queries, keys, values, grad_out, row_lse, row_delta, doc_ids, pairs):
    rows, qh, hd = queries.shape
    kvh = keys.shape[1]
    grp = qh // kvh
    spans = zs * ss
    stripe = rows // spans
    chunks = 2 * kvh
    vm = pl.BlockSpec(memory_space=pltpu.VMEM)
    sm = pl.BlockSpec(memory_space=pltpu.SMEM)
    hbm = pl.BlockSpec(memory_space=pltpu.HBM)
    dma = pltpu.SemaphoreType.DMA
    dq, dk, dv = pl.pallas_call(
        functools.partial(kernel, (zs, ss, rows, kvh, grp, hd)),
        out_shape=(
            pltpu.VMEM((rows, qh, hd), F32),
            pltpu.VMEM((rows * kvh, hd), F32),
            pltpu.VMEM((rows * kvh, hd), F32),
        ),
        in_specs=[sm, hbm, hbm, hbm, hbm, hbm, hbm, hbm],
        out_specs=(vm, vm, vm),
        scratch_shapes=[
            pltpu.VMEM((1, rows), jnp.int32),
            pltpu.VMEM((qh, rows), F32),
            pltpu.VMEM((qh, rows), F32),
            pltpu.VMEM((rows * kvh, hd), BF),
            pltpu.VMEM((rows * kvh, hd), BF),
            pltpu.VMEM((rows, qh, hd), BF),
            pltpu.VMEM((rows, qh, hd), BF),
            pltpu.VMEM((kvh, rows * grp, 2 * hd), BF),
            pltpu.VMEM((kvh, rows * grp, 2 * hd), BF),
            pltpu.VMEM((rows, rows), F32),
            pltpu.VMEM((2 * rows, 2 * hd), BF),
            pltpu.VMEM((2 * rows, 2 * hd), BF),
            pltpu.VMEM((rows, 2 * hd), BF),
            pltpu.VMEM((rows, 2 * hd), BF),
            pltpu.VMEM((rows * grp, 2 * rows), F32),
            pltpu.VMEM((kvh, rows, hd), F32),
            pltpu.VMEM((kvh, rows, hd), F32),
            [pltpu.VMEM((spans, rows, hd), BF) for _ in range(chunks)],
            pltpu.VMEM((chunks * spans, 2, stripe, hd), BF),
            pltpu.VMEM((chunks * spans, 2, stripe, hd), BF),
            pltpu.VMEM((chunks * spans, stripe, hd), BF),
            pltpu.VMEM((chunks * spans, stripe, hd), BF),
            dma((7,)),
            dma((chunks, 2)),
            dma((chunks,)),
            dma((chunks, zs)),
            dma((chunks,)),
            dma((1,)),
            dma((chunks,)),
            dma((1,)),
            dma((chunks,)),
        ],
        compiler_params=pltpu.CompilerParams(collective_id=0, has_side_effects=True),
        name="span_grads",
    )(
        pairs.T, doc_ids.reshape(1, rows), row_lse.T, row_delta.T,
        keys.reshape(rows * kvh, hd), values.reshape(rows * kvh, hd), queries, grad_out,
    )
    dq, dk, dv = written(dq, dk, dv)
    return dq, dk.reshape(rows, kvh, hd), dv.reshape(rows, kvh, hd)


QH = 64
KVH = 4


def block_terms(query_blk, upstream, log_norm, row_terms, key_blk, value_blk, allowed, factor):
    scores = (
        jnp.einsum("tghd,kgd->tghk", query_blk, key_blk, preferred_element_type=jnp.float32)
        * factor
    )
    probs = jnp.exp(scores - log_norm[..., None])
    if allowed is not None:
        probs = jnp.where(allowed[:, None, None, :], probs, 0.0)
    grad_probs = jnp.einsum(
        "tghd,kgd->tghk", upstream, value_blk, preferred_element_type=jnp.float32
    )
    grad_scores = probs * (grad_probs - row_terms[..., None])
    probs_low = probs.astype(jnp.bfloat16)
    scores_low = grad_scores.astype(jnp.bfloat16)
    grad_val = jnp.einsum("tghk,tghd->kgd", probs_low, upstream, preferred_element_type=jnp.float32)
    grad_key = (
        jnp.einsum("tghk,tghd->kgd", scores_low, query_blk, preferred_element_type=jnp.float32)
        * factor
    )
    grad_query = (
        jnp.einsum("tghk,kgd->tghd", scores_low, key_blk, preferred_element_type=jnp.float32)
        * factor
    )
    return (grad_query, grad_key, grad_val)


def body(zs, ss, queries, keys, values, grad_out, row_lse, row_delta, doc_ids, pairs):
    grp = queries.shape[1] // keys.shape[1]
    if (
        ss == 2
        and queries.shape[0] % (16 * zs * ss) == 0
        and grp % 16 == 0
        and 3 * queries.shape[1] <= queries.shape[2]
    ):
        return fused(
            zs, ss, queries, keys, values, grad_out, row_lse, row_delta, doc_ids, pairs
        )
    rows_here = queries.shape[0]
    heads_here = keys.shape[1]
    head_dim = keys.shape[2]
    grouped = QH // KVH
    factor = head_dim ** (-0.5)
    spans = lax.axis_size(("ctx", "sub"))
    stripe = rows_here // spans
    query_blk = queries.reshape(rows_here, heads_here, grouped, head_dim)
    upstream = grad_out.reshape(rows_here, heads_here, grouped, head_dim)
    log_norm = row_lse.reshape(rows_here, heads_here, grouped)
    row_terms = row_delta.reshape(rows_here, heads_here, grouped)
    positions = jnp.arange(rows_here, dtype=jnp.int32)
    allowed = (positions[:, None] >= positions[None, :]) & (doc_ids[:, None] == doc_ids[None, :])
    query_sum, key_local, value_local = block_terms(
        query_blk, upstream, log_norm, row_terms, keys, values, allowed, factor
    )
    stacked = jnp.concatenate([keys, values], axis=2).reshape(rows_here, heads_here * 2 * head_dim)
    features = stacked.shape[1]
    spread = lax.all_to_all(
        stacked.reshape(spans, stripe, features),
        ("ctx", "sub"),
        split_axis=0,
        concat_axis=0,
        tiled=True,
    )
    wanted = jnp.take(spread, pairs.T, axis=0)
    remote = lax.all_to_all(
        wanted, ("ctx", "sub"), split_axis=1, concat_axis=1, tiled=True
    ).reshape(2, rows_here, features)
    remote = remote.reshape(2, rows_here, heads_here, 2 * head_dim)
    returned = []
    for which in range(2):
        far_keys = remote[which, :, :, :head_dim]
        far_values = remote[which, :, :, head_dim:]
        query_part, key_part, value_part = block_terms(
            query_blk, upstream, log_norm, row_terms, far_keys, far_values, None, factor
        )
        query_sum = query_sum + query_part
        returned.append(
            jnp.concatenate([key_part, value_part], axis=2).reshape(rows_here, features)
        )
    outgoing = jnp.stack(returned).reshape(2, spans, stripe, features)
    incoming = lax.all_to_all(outgoing, ("ctx", "sub"), split_axis=1, concat_axis=1, tiled=True)
    owners = pairs.T.reshape(-1)
    select = (jnp.arange(spans, dtype=jnp.int32)[:, None] == owners[None, :]).astype(jnp.float32)
    summed = jnp.dot(
        select,
        incoming.reshape(2 * spans, stripe * features),
        precision=lax.Precision.HIGHEST,
        preferred_element_type=jnp.float32,
    )
    at_home = lax.all_to_all(
        summed.reshape(spans, stripe, features),
        ("ctx", "sub"),
        split_axis=0,
        concat_axis=0,
        tiled=True,
    )
    at_home = at_home.reshape(rows_here, heads_here, 2 * head_dim)
    grad_keys = key_local + at_home[:, :, :head_dim]
    grad_values = value_local + at_home[:, :, head_dim:]
    grad_queries = query_sum.reshape(rows_here, heads_here * grouped, head_dim)
    return (grad_queries, grad_keys, grad_values)


def solution(mesh):
    return jax.shard_map(
        functools.partial(body, mesh.shape["ctx"], mesh.shape["sub"]),
        mesh=mesh,
        in_specs=(
            P(("groups", "ctx", "sub"), "head", None),
            P(("groups", "ctx", "sub"), "head", None),
            P(("groups", "ctx", "sub"), "head", None),
            P(("groups", "ctx", "sub"), "head", None),
            P(("groups", "ctx", "sub"), "head"),
            P(("groups", "ctx", "sub"), "head"),
            P(("groups", "ctx", "sub")),
            P("groups", None),
        ),
        out_specs=(
            P(("groups", "ctx", "sub"), "head", None),
            P(("groups", "ctx", "sub"), "head", None),
            P(("groups", "ctx", "sub"), "head", None),
        ),
        check_vma=False,
    )
```

time: 32.6 us -> 30.8 us (0.945)
  Pallas kernels: 31.7 us -> 30 us
    pallas_call x1, Pallas kernels: 30.3 us -> 28.6 us  [fused(): pl.pallas_call(functools.partial(kernel, (zs, ss, rows, kvh, grp, hd)), o...]
where the time goes in v2:
time: 30.8 us; the launch traced here: 30.6 us
  Pallas kernels  30 us (97%)
  between operations  0.64 us (2%)
    pallas_call x1, Pallas kernels, fused(): pl.pallas_call(functools.partial(kernel, (zs, ss, rows, kvh, grp, hd)), o...  28.6 us
    pallas_call x1, Pallas kernels, written(): pl.pallas_call(tail_kernel, out_shape=tuple((jax.ShapeDtypeStruct(x.shape...  1.42 us

profile of v2, /device:TPU:0, one launch (start us, length us, event | category | flops | bytes accessed | tf_op | source)
XLA Modules:
  0.0 30.6 jit_solution(11355013055174847427)
XLA Ops:
  0.6 28.6 %span_grads.1 = (f32[128,32,128]{2,1,0:T(8,128)S(1)}, f32[256,128]{1,0:T(8,128)S(1)}, f32[256,128]{1,0:T(8,128)S(1)}) custom-call(s32[2,8]{1,0:T(2,128)} %bitcast.12, s32[1,128]{1,0:T(1,128)} %bitcast.13, f32[32,128]{1,0:T(8,128)} %bitcast.10, f32[32,128]{1,0:T(8,128)} %bitcast.11, bf16[256,128]{1,0:T(8,128)(2,1)} %bitcast.8, bf16[256,128]{1,0:T(8,128)(2,1)} %bitcast.9, ...), custom_call_target="tpu_custom_call" | custom-call | tf_op jit(solution)/shard_map/span_grads/pallas_call | solution.py:339
  29.2 1.4 %write_out.1 = (f32[128,32,128]{2,1,0:T(8,128)}, f32[256,128]{1,0:T(8,128)}, f32[256,128]{1,0:T(8,128)}) custom-call(f32[128,32,128]{2,1,0:T(8,128)S(1)} %get-tuple-element.9.dq_vm, f32[256,128]{1,0:T(8,128)S(1)} %get-tuple-element.10.dk_vm, f32[256,128]{1,0:T(8,128)S(1)} %get-tuple-element.11.dv_vm), custom_call_target="tpu_custom_call" | custom-call | tf_op jit(solution)/shard_map/write_out/pallas_call | solution.py:317

commit v3 on v2

--- a/solution.py
+++ b/solution.py
@@ -26,7 +26,7 @@
     pairs_ref, docs_hbm, lse_hbm, delta_hbm, keys_hbm, vals_hbm, q_hbm, up_hbm,
     dq_vm, dk_ref, dv_ref,
     docs_ref, lse_ref, delta_ref, keys_ref, vals_ref, q_vm, up_vm,
-    qa, da, bias, kfar, vfar, kloc, vloc, probs,
+    qa, da, bias, kfar, vfar, kloc, vloc, wide,
     dk_loc, dv_loc, kv, send_a, recv_a, send_b, recv_b,
     in_sem, z_send, p_send, z_recv, p_recv, a_send, a_recv, b_send, b_recv,
 ):
@@ -43,6 +43,7 @@
     mine = s * zs + z
     nt = (((1,), (1,)), ((), ()))
     tn = (((0,), (0,)), ((), ()))
+    direct = [hop for hop in (2, 1) if hop < zs]
 
     barrier = pltpu.get_barrier_semaphore()
 
@@ -51,13 +52,14 @@
 
     greet(z, other)
 
-    @pl.when(z > 0)
-    def _():
-        greet(z - 1, s)
-
-    @pl.when(z < zs - 1)
-    def _():
-        greet(z + 1, s)
+    for hop in direct:
+        @pl.when(z >= hop)
+        def _():
+            greet(z - hop, s)
+
+        @pl.when(z + hop < zs)
+        def _():
+            greet(z + hop, s)
 
     ins = [
         pltpu.make_async_copy(src, dst, in_sem.at[i])
@@ -66,19 +68,15 @@
             (docs_hbm, docs_ref), (q_hbm, q_vm), (up_hbm, up_vm),
         ))
     ]
-    for c in ins:
+    for c in ins[:5]:
         c.start()
-
-    pick_t = lax.broadcasted_iota(jnp.int32, (rows, rows * kvh), 0)
-    pick_r = lax.broadcasted_iota(jnp.int32, (rows, rows * kvh), 1)
     for part, ref in enumerate((keys_ref, vals_ref)):
         ins[part].wait()
+        wide[part] = ref[...].astype(F32)
         for g in range(kvh):
-            pick = jnp.where(pick_r == pick_t * kvh + g, 1.0, 0.0).astype(BF)
-            took = jnp.dot(pick, ref[...], preferred_element_type=F32)
-            kv[g * 2 + part][mine] = took.astype(BF)
-
-    ends = jnp.where(z > 0, 1, 0) + jnp.where(z < zs - 1, 1, 0)
+            kv[g * 2 + part][mine] = wide[part, pl.ds(g, rows, stride=kvh), :].astype(BF)
+
+    ends = sum(jnp.where(z >= hop, 1, 0) + jnp.where(z + hop < zs, 1, 0) for hop in direct)
     pl.semaphore_wait(barrier, 1 + ends)
 
     def to_line(c, slot, from_z, dz, way):
@@ -94,13 +92,14 @@
             device_id={"ctx": z, "sub": other}, device_id_type=MESH)
 
     def own_step(c):
-        @pl.when(z < zs - 1)
-        def _():
-            to_line(c, mine, z, z + 1, 0).start()
-
-        @pl.when(z > 0)
-        def _():
-            to_line(c, mine, z, z - 1, 1).start()
+        for hop in direct:
+            @pl.when(z + hop < zs)
+            def _():
+                to_line(c, mine, z, z + hop, 0).start()
+
+            @pl.when(z >= hop)
+            def _():
+                to_line(c, mine, z, z - hop, 1).start()
 
         to_partner(c, mine).start()
 
@@ -110,7 +109,7 @@
             slot = mine - j
             to_line(c, slot, z - j, z, 0).wait_recv()
 
-            @pl.when(z < zs - 1)
+            @pl.when((z < zs - 1) & (j >= len(direct)))
             def _():
                 to_line(c, slot, z - j, z + 1, 0).start()
 
@@ -121,7 +120,7 @@
             slot = mine + j
             to_line(c, slot, z + j, z, 1).wait_recv()
 
-            @pl.when(z > 0)
+            @pl.when((z > 0) & (j >= len(direct)))
             def _():
                 to_line(c, slot, z + j, z - 1, 1).start()
 
@@ -131,15 +130,19 @@
         for at in range(zs):
             @pl.when(z == at)
             def _():
-                if at < zs - 1:
-                    to_line(c, pl.ds(0, at + 1), at, z, 0).wait_send()
-                if at > 0:
-                    to_line(c, pl.ds(0, zs - at), at, z, 1).wait_send()
+                for way, behind in enumerate((at, zs - 1 - at)):
+                    ahead = zs - 1 - behind
+                    count = min(ahead, len(direct))
+                    if ahead > 0:
+                        count += max(0, behind - len(direct) + 1)
+                        to_line(c, pl.ds(0, count), at, z, way).wait_send()
 
         to_partner(c, pl.ds(0, zs)).wait_send()
 
     for c in range(chunks):
         own_step(c)
+    for c in ins[5:]:
+        c.start()
 
     for c in ins[2:5]:
         c.wait()
@@ -218,21 +221,20 @@
                 send_sem=a_send.at[0], recv_sem=a_recv.at[c],
                 device_id=at, device_id_type=MESH).start()
 
-    def far_keys(g):
+    def far(g):
         listed(g * 2, kfar)
+        listed(g * 2 + 1, vfar)
         x = lax.dot_general(qa[g], kfar[...], nt, preferred_element_type=F32)
+        y = lax.dot_general(da[g], vfar[...], nt, preferred_element_type=F32)
         p = jnp.exp2(x * scale2)
-        probs[...] = p
-        give(g * 2 + 1, lax.dot_general(p.astype(BF), da[g, :, :hd], tn, preferred_element_type=F32))
-
-    def far_vals(g):
-        listed(g * 2 + 1, vfar)
-        y = lax.dot_general(da[g], vfar[...], nt, preferred_element_type=F32)
-        ds_low = (probs[...] * y).astype(BF)
-        give(g * 2, lax.dot_general(ds_low, qa[g, :, :hd], tn, preferred_element_type=F32))
+        ds_low = (p * y).astype(BF)
         dq = jnp.dot(ds_low, kfar[:, :hd], preferred_element_type=F32).reshape(rows, grp, hd)
+        dk = lax.dot_general(ds_low, qa[g, :, :hd], tn, preferred_element_type=F32)
+        dv = lax.dot_general(p.astype(BF), da[g, :, :hd], tn, preferred_element_type=F32)
         sl = pl.ds(g * grp, grp)
         dq_vm[:, sl, :] = (dq_vm[:, sl, :] + dq) * factor
+        give(g * 2 + 1, dv)
+        give(g * 2, dk)
 
     def many(ref, first, count, send_sem, recv_sem):
         return pltpu.make_async_remote_copy(
@@ -274,23 +276,21 @@
     def partner_wait(c):
         to_partner(c, pl.ds(other * zs, zs)).wait_recv()
 
+    last = zs - 1
     for g in range(kvh):
         near(g)
-        relay_step(g * 2, 1)
-        relay_step(g * 2 + 1, 1)
-    for j in range(2, zs - 1):
+        for c in ([0] if g == 0 else []) + (list(range(1, chunks)) if g == kvh - 1 else []):
+            for j in range(1, min(last, len(direct) + 1)):
+                relay_step(c, j)
+    for j in range(len(direct) + 1, last):
         for c in range(chunks):
             relay_step(c, j)
-
-    last = zs - 1
-    if last > 1:
-        relay_step(0, last)
-        relay_step(1, last)
-    for c in range(chunks):
-        partner_wait(c)
-        (far_keys if c % 2 == 0 else far_vals)(c // 2)
-        if last > 1 and c + 2 < chunks:
-            relay_step(c + 2, last)
+    for g in range(kvh):
+        for c in (g * 2, g * 2 + 1):
+            relay_step(c, last)
+        for c in (g * 2, g * 2 + 1):
+            partner_wait(c)
+        far(g)
     order = [g * 2 + part for g in range(kvh) for part in (1, 0)]
     for c in order:
         combine(c)
@@ -360,7 +360,7 @@
             pltpu.VMEM((2 * rows, 2 * hd), BF),
             pltpu.VMEM((rows, 2 * hd), BF),
             pltpu.VMEM((rows, 2 * hd), BF),
-            pltpu.VMEM((rows * grp, 2 * rows), F32),
+            pltpu.VMEM((2, rows * kvh, hd), F32),
             pltpu.VMEM((kvh, rows, hd), F32),
             pltpu.VMEM((kvh, rows, hd), F32),
             [pltpu.VMEM((spans, rows, hd), BF) for _ in range(chunks)],

time: 30.8 us -> 32.1 us (1.042)
  Pallas kernels: 30 us -> 31.2 us
    pallas_call x1, Pallas kernels: 28.6 us -> 29.8 us  [fused(): pl.pallas_call(functools.partial(kernel, (zs, ss, rows, kvh, grp, hd)), o...]
where the time goes in v3:
time: 32.1 us; the launch traced here: 31.9 us
  Pallas kernels  31.2 us (97%)
  between operations  0.64 us (2%)
    pallas_call x1, Pallas kernels, fused(): pl.pallas_call(functools.partial(kernel, (zs, ss, rows, kvh, grp, hd)), o...  29.8 us
    pallas_call x1, Pallas kernels, written(): pl.pallas_call(tail_kernel, out_shape=tuple((jax.ShapeDtypeStruct(x.shape...  1.42 us

profile of v3, /device:TPU:0, one launch (start us, length us, event | category | flops | bytes accessed | tf_op | source)
XLA Modules:
  0.0 31.9 jit_solution(7553135994136208047)
XLA Ops:
  0.6 29.8 %span_grads.1 = (f32[128,32,128]{2,1,0:T(8,128)S(1)}, f32[256,128]{1,0:T(8,128)S(1)}, f32[256,128]{1,0:T(8,128)S(1)}) custom-call(s32[2,8]{1,0:T(2,128)} %bitcast.12, s32[1,128]{1,0:T(1,128)} %bitcast.13, f32[32,128]{1,0:T(8,128)} %bitcast.10, f32[32,128]{1,0:T(8,128)} %bitcast.11, bf16[256,128]{1,0:T(8,128)(2,1)} %bitcast.8, bf16[256,128]{1,0:T(8,128)(2,1)} %bitcast.9, ...), custom_call_target="tpu_custom_call" | custom-call | tf_op jit(solution)/shard_map/span_grads/pallas_call | solution.py:339
  30.4 1.4 %write_out.1 = (f32[128,32,128]{2,1,0:T(8,128)}, f32[256,128]{1,0:T(8,128)}, f32[256,128]{1,0:T(8,128)}) custom-call(f32[128,32,128]{2,1,0:T(8,128)S(1)} %get-tuple-element.9.dq_vm, f32[256,128]{1,0:T(8,128)S(1)} %get-tuple-element.10.dk_vm, f32[256,128]{1,0:T(8,128)S(1)} %get-tuple-element.11.dv_vm), custom_call_target="tpu_custom_call" | custom-call | tf_op jit(solution)/shard_map/write_out/pallas_call | solution.py:317

commit v4 on v2

--- a/solution.py
+++ b/solution.py
@@ -23,10 +23,10 @@
 
 def kernel(
     dims,
-    pairs_ref, docs_hbm, lse_hbm, delta_hbm, keys_hbm, vals_hbm, q_hbm, up_hbm,
+    pairs_hbm, docs_hbm, lse_hbm, delta_hbm, keys_hbm, vals_hbm, q_hbm, up_hbm,
     dq_vm, dk_ref, dv_ref,
-    docs_ref, lse_ref, delta_ref, keys_ref, vals_ref, q_vm, up_vm,
-    qa, da, bias, kfar, vfar, kloc, vloc, probs,
+    pairs_ref, docs_ref, lse_ref, delta_ref, keys_ref, vals_ref, q_vm, up_vm,
+    qa, da, bias, kfar, vfar, kloc, vloc, wide, probs,
     dk_loc, dv_loc, kv, send_a, recv_a, send_b, recv_b,
     in_sem, z_send, p_send, z_recv, p_recv, a_send, a_recv, b_send, b_recv,
 ):
@@ -63,20 +63,18 @@
         pltpu.make_async_copy(src, dst, in_sem.at[i])
         for i, (src, dst) in enumerate((
             (keys_hbm, keys_ref), (vals_hbm, vals_ref), (lse_hbm, lse_ref), (delta_hbm, delta_ref),
-            (docs_hbm, docs_ref), (q_hbm, q_vm), (up_hbm, up_vm),
+            (docs_hbm, docs_ref), (pairs_hbm, pairs_ref), (q_hbm, q_vm), (up_hbm, up_vm),
         ))
     ]
-    for c in ins:
+    for c in ins[:6]:
         c.start()
-
-    pick_t = lax.broadcasted_iota(jnp.int32, (rows, rows * kvh), 0)
-    pick_r = lax.broadcasted_iota(jnp.int32, (rows, rows * kvh), 1)
     for part, ref in enumerate((keys_ref, vals_ref)):
         ins[part].wait()
+        wide[part] = ref[...].astype(F32)
         for g in range(kvh):
-            pick = jnp.where(pick_r == pick_t * kvh + g, 1.0, 0.0).astype(BF)
-            took = jnp.dot(pick, ref[...], preferred_element_type=F32)
-            kv[g * 2 + part][mine] = took.astype(BF)
+            kv[g * 2 + part][mine] = wide[part, pl.ds(g, rows, stride=kvh), :].astype(BF)
+    for c in ins[6:]:
+        c.start()
 
     ends = jnp.where(z > 0, 1, 0) + jnp.where(z < zs - 1, 1, 0)
     pl.semaphore_wait(barrier, 1 + ends)
@@ -138,10 +136,10 @@
 
         to_partner(c, pl.ds(0, zs)).wait_send()
 
-    for c in range(chunks):
+    for c in range(2):
         own_step(c)
 
-    for c in ins[2:5]:
+    for c in ins[2:6]:
         c.wait()
     pos_t = lax.broadcasted_iota(jnp.int32, (rows, rows), 0)
     pos_u = lax.broadcasted_iota(jnp.int32, (rows, rows), 1)
@@ -172,7 +170,7 @@
         js = slice(j * rows, (j + 1) * rows)
         kfar[js, hd:] = neg
         vfar[js, hd:] = neg
-    for c in ins[5:]:
+    for c in ins[6:]:
         c.wait()
 
     def near(g):
@@ -234,6 +232,21 @@
         sl = pl.ds(g * grp, grp)
         dq_vm[:, sl, :] = (dq_vm[:, sl, :] + dq) * factor
 
+    def far(g):
+        listed(g * 2, kfar)
+        listed(g * 2 + 1, vfar)
+        x = lax.dot_general(qa[g], kfar[...], nt, preferred_element_type=F32)
+        y = lax.dot_general(da[g], vfar[...], nt, preferred_element_type=F32)
+        p = jnp.exp2(x * scale2)
+        ds_low = (p * y).astype(BF)
+        dq = jnp.dot(ds_low, kfar[:, :hd], preferred_element_type=F32).reshape(rows, grp, hd)
+        dk = lax.dot_general(ds_low, qa[g, :, :hd], tn, preferred_element_type=F32)
+        dv = lax.dot_general(p.astype(BF), da[g, :, :hd], tn, preferred_element_type=F32)
+        sl = pl.ds(g * grp, grp)
+        dq_vm[:, sl, :] = (dq_vm[:, sl, :] + dq) * factor
+        give(g * 2 + 1, dv)
+        give(g * 2, dk)
+
     def many(ref, first, count, send_sem, recv_sem):
         return pltpu.make_async_remote_copy(
             src_ref=ref.at[pl.ds(first, count)], dst_ref=ref.at[pl.ds(first, count)],
@@ -274,23 +287,31 @@
     def partner_wait(c):
         to_partner(c, pl.ds(other * zs, zs)).wait_recv()
 
+    last = zs - 1
     for g in range(kvh):
         near(g)
+        if g == 0:
+            for c in range(2, chunks):
+                own_step(c)
         relay_step(g * 2, 1)
         relay_step(g * 2 + 1, 1)
-    for j in range(2, zs - 1):
+    for j in range(2, last):
         for c in range(chunks):
             relay_step(c, j)
-
-    last = zs - 1
     if last > 1:
         relay_step(0, last)
         relay_step(1, last)
-    for c in range(chunks):
-        partner_wait(c)
-        (far_keys if c % 2 == 0 else far_vals)(c // 2)
-        if last > 1 and c + 2 < chunks:
-            relay_step(c + 2, last)
+    for g in range(kvh - 1):
+        partner_wait(g * 2)
+        partner_wait(g * 2 + 1)
+        far(g)
+        if last > 1:
+            relay_step(g * 2 + 2, last)
+            relay_step(g * 2 + 3, last)
+    partner_wait(chunks - 2)
+    far_keys(kvh - 1)
+    partner_wait(chunks - 1)
+    far_vals(kvh - 1)
     order = [g * 2 + part for g in range(kvh) for part in (1, 0)]
     for c in order:
         combine(c)
@@ -333,7 +354,6 @@
     stripe = rows // spans
     chunks = 2 * kvh
     vm = pl.BlockSpec(memory_space=pltpu.VMEM)
-    sm = pl.BlockSpec(memory_space=pltpu.SMEM)
     hbm = pl.BlockSpec(memory_space=pltpu.HBM)
     dma = pltpu.SemaphoreType.DMA
     dq, dk, dv = pl.pallas_call(
@@ -343,9 +363,10 @@
             pltpu.VMEM((rows * kvh, hd), F32),
             pltpu.VMEM((rows * kvh, hd), F32),
         ),
-        in_specs=[sm, hbm, hbm, hbm, hbm, hbm, hbm, hbm],
+        in_specs=[hbm, hbm, hbm, hbm, hbm, hbm, hbm, hbm],
         out_specs=(vm, vm, vm),
         scratch_shapes=[
+            pltpu.SMEM(pairs.shape[::-1], jnp.int32),
             pltpu.VMEM((1, rows), jnp.int32),
             pltpu.VMEM((qh, rows), F32),
             pltpu.VMEM((qh, rows), F32),
@@ -360,6 +381,7 @@
             pltpu.VMEM((2 * rows, 2 * hd), BF),
             pltpu.VMEM((rows, 2 * hd), BF),
             pltpu.VMEM((rows, 2 * hd), BF),
+            pltpu.VMEM((2, rows * kvh, hd), F32),
             pltpu.VMEM((rows * grp, 2 * rows), F32),
             pltpu.VMEM((kvh, rows, hd), F32),
             pltpu.VMEM((kvh, rows, hd), F32),
@@ -368,7 +390,7 @@
             pltpu.VMEM((chunks * spans, 2, stripe, hd), BF),
             pltpu.VMEM((chunks * spans, stripe, hd), BF),
             pltpu.VMEM((chunks * spans, stripe, hd), BF),
-            dma((7,)),
+            dma((8,)),
             dma((chunks, 2)),
             dma((chunks,)),
             dma((chunks, zs)),

time: 30.8 us -> 30.5 us (level)
  no operation moved by 1% of the time
where the time goes in v4:
time: 30.5 us; the launch traced here: 30.4 us
  Pallas kernels  29.7 us (97%)
  between operations  0.64 us (2%)
    pallas_call x1, Pallas kernels, fused(): pl.pallas_call(functools.partial(kernel, (zs, ss, rows, kvh, grp, hd)), o...  28.3 us
    pallas_call x1, Pallas kernels, written(): pl.pallas_call(tail_kernel, out_shape=tuple((jax.ShapeDtypeStruct(x.shape...  1.42 us

profile of v4, /device:TPU:0, one launch (start us, length us, event | category | flops | bytes accessed | tf_op | source)
XLA Modules:
  0.0 30.4 jit_solution(9312168533896739801)
XLA Ops:
  0.6 28.3 %span_grads.1 = (f32[128,32,128]{2,1,0:T(8,128)S(1)}, f32[256,128]{1,0:T(8,128)S(1)}, f32[256,128]{1,0:T(8,128)S(1)}) custom-call(s32[2,8]{1,0:T(2,128)} %bitcast.12, s32[1,128]{1,0:T(1,128)} %bitcast.13, f32[32,128]{1,0:T(8,128)} %bitcast.10, f32[32,128]{1,0:T(8,128)} %bitcast.11, bf16[256,128]{1,0:T(8,128)(2,1)} %bitcast.8, bf16[256,128]{1,0:T(8,128)(2,1)} %bitcast.9, ...), custom_call_target="tpu_custom_call" | custom-call | tf_op jit(solution)/shard_map/span_grads/pallas_call | solution.py:359
  29.0 1.4 %write_out.1 = (f32[128,32,128]{2,1,0:T(8,128)}, f32[256,128]{1,0:T(8,128)}, f32[256,128]{1,0:T(8,128)}) custom-call(f32[128,32,128]{2,1,0:T(8,128)S(1)} %get-tuple-element.9.dq_vm, f32[256,128]{1,0:T(8,128)S(1)} %get-tuple-element.10.dk_vm, f32[256,128]{1,0:T(8,128)S(1)} %get-tuple-element.11.dv_vm), custom_call_target="tpu_custom_call" | custom-call | tf_op jit(solution)/shard_map/write_out/pallas_call | solution.py:338

commit v5 on v4

--- a/solution.py
+++ b/solution.py
@@ -136,7 +136,7 @@
 
         to_partner(c, pl.ds(0, zs)).wait_send()
 
-    for c in range(2):
+    for c in range(chunks):
         own_step(c)
 
     for c in ins[2:6]:
@@ -291,23 +291,27 @@
     for g in range(kvh):
         near(g)
         if g == 0:
-            for c in range(2, chunks):
-                own_step(c)
-        relay_step(g * 2, 1)
-        relay_step(g * 2 + 1, 1)
+            for c in range(chunks):
+                relay_step(c, 1)
     for j in range(2, last):
         for c in range(chunks):
             relay_step(c, j)
     if last > 1:
         relay_step(0, last)
         relay_step(1, last)
+
+    def next_two(g, core):
+        @pl.when((s == core) & (last > 1))
+        def _():
+            relay_step(g * 2 + 2, last)
+            relay_step(g * 2 + 3, last)
+
     for g in range(kvh - 1):
+        next_two(g, ss - 1)
         partner_wait(g * 2)
         partner_wait(g * 2 + 1)
         far(g)
-        if last > 1:
-            relay_step(g * 2 + 2, last)
-            relay_step(g * 2 + 3, last)
+        next_two(g, 0)
     partner_wait(chunks - 2)
     far_keys(kvh - 1)
     partner_wait(chunks - 1)

time: 30.5 us -> 29.4 us (0.964)
  Pallas kernels: 29.7 us -> 28.6 us
    pallas_call x1, Pallas kernels: 28.3 us -> 27.2 us  [fused(): pl.pallas_call(functools.partial(kernel, (zs, ss, rows, kvh, grp, hd)), o...]
where the time goes in v5:
time: 29.4 us; the launch traced here: 29.3 us
  Pallas kernels  28.6 us (97%)
  between operations  0.64 us (2%)
    pallas_call x1, Pallas kernels, fused(): pl.pallas_call(functools.partial(kernel, (zs, ss, rows, kvh, grp, hd)), o...  27.2 us
    pallas_call x1, Pallas kernels, written(): pl.pallas_call(tail_kernel, out_shape=tuple((jax.ShapeDtypeStruct(x.shape...  1.42 us

profile of v5, /device:TPU:0, one launch (start us, length us, event | category | flops | bytes accessed | tf_op | source)
XLA Modules:
  0.0 29.3 jit_solution(3000520417924650330)
XLA Ops:
  0.6 27.2 %span_grads.1 = (f32[128,32,128]{2,1,0:T(8,128)S(1)}, f32[256,128]{1,0:T(8,128)S(1)}, f32[256,128]{1,0:T(8,128)S(1)}) custom-call(s32[2,8]{1,0:T(2,128)} %bitcast.12, s32[1,128]{1,0:T(1,128)} %bitcast.13, f32[32,128]{1,0:T(8,128)} %bitcast.10, f32[32,128]{1,0:T(8,128)} %bitcast.11, bf16[256,128]{1,0:T(8,128)(2,1)} %bitcast.8, bf16[256,128]{1,0:T(8,128)(2,1)} %bitcast.9, ...), custom_call_target="tpu_custom_call" | custom-call | tf_op jit(solution)/shard_map/span_grads/pallas_call | solution.py:363
  27.9 1.4 %write_out.1 = (f32[128,32,128]{2,1,0:T(8,128)}, f32[256,128]{1,0:T(8,128)}, f32[256,128]{1,0:T(8,128)}) custom-call(f32[128,32,128]{2,1,0:T(8,128)S(1)} %get-tuple-element.9.dq_vm, f32[256,128]{1,0:T(8,128)S(1)} %get-tuple-element.10.dk_vm, f32[256,128]{1,0:T(8,128)S(1)} %get-tuple-element.11.dv_vm), custom_call_target="tpu_custom_call" | custom-call | tf_op jit(solution)/shard_map/write_out/pallas_call | solution.py:342

commit v6 on v5

--- a/solution.py
+++ b/solution.py
@@ -43,6 +43,7 @@
     mine = s * zs + z
     nt = (((1,), (1,)), ((), ()))
     tn = (((0,), (0,)), ((), ()))
+    skip = zs > 3
 
     barrier = pltpu.get_barrier_semaphore()
 
@@ -58,6 +59,15 @@
     @pl.when(z < zs - 1)
     def _():
         greet(z + 1, s)
+
+    if skip:
+        @pl.when(z == 2)
+        def _():
+            greet(0, s)
+
+        @pl.when(z == zs - 3)
+        def _():
+            greet(zs - 1, s)
 
     ins = [
         pltpu.make_async_copy(src, dst, in_sem.at[i])
@@ -77,6 +87,8 @@
         c.start()
 
     ends = jnp.where(z > 0, 1, 0) + jnp.where(z < zs - 1, 1, 0)
+    if skip:
+        ends = ends + jnp.where((z == 0) | (z == zs - 1), 1, 0)
     pl.semaphore_wait(barrier, 1 + ends)
 
     def to_line(c, slot, from_z, dz, way):
@@ -92,6 +104,15 @@
             device_id={"ctx": z, "sub": other}, device_id_type=MESH)
 
     def own_step(c):
+        if skip:
+            @pl.when(z == 0)
+            def _():
+                to_line(c, mine, z, 2, 0).start()
+
+            @pl.when(z == zs - 1)
+            def _():
+                to_line(c, mine, z, zs - 3, 1).start()
+
         @pl.when(z < zs - 1)
         def _():
             to_line(c, mine, z, z + 1, 0).start()
@@ -108,7 +129,7 @@
             slot = mine - j
             to_line(c, slot, z - j, z, 0).wait_recv()
 
-            @pl.when(z < zs - 1)
+            @pl.when((z < zs - 1) & ((z > 1) | (not skip)))
             def _():
                 to_line(c, slot, z - j, z + 1, 0).start()
 
@@ -119,7 +140,7 @@
             slot = mine + j
             to_line(c, slot, z + j, z, 1).wait_recv()
 
-            @pl.when(z > 0)
+            @pl.when((z > 0) & ((z < zs - 2) | (not skip)))
             def _():
                 to_line(c, slot, z + j, z - 1, 1).start()
 
@@ -129,10 +150,12 @@
         for at in range(zs):
             @pl.when(z == at)
             def _():
-                if at < zs - 1:
-                    to_line(c, pl.ds(0, at + 1), at, z, 0).wait_send()
-                if at > 0:
-                    to_line(c, pl.ds(0, zs - at), at, z, 1).wait_send()
+                for way, behind in enumerate((at, zs - 1 - at)):
+                    count = behind + 1
+                    if skip:
+                        count += (behind == 0) - (behind == 1)
+                    if behind < zs - 1:
+                        to_line(c, pl.ds(0, count), at, z, way).wait_send()
 
         to_partner(c, pl.ds(0, zs)).wait_send()
 
@@ -288,13 +311,23 @@
         to_partner(c, pl.ds(other * zs, zs)).wait_recv()
 
     last = zs - 1
+    middle = (z > 0) & (z < last)
+
+    def second(where):
+        @pl.when(where & (last > 2))
+        def _():
+            relay_step(0, 2)
+            relay_step(1, 2)
+
     for g in range(kvh):
         near(g)
         if g == 0:
             for c in range(chunks):
                 relay_step(c, 1)
+            second(middle)
+    second(jnp.logical_not(middle))
     for j in range(2, last):
-        for c in range(chunks):
+        for c in range(2 if j == 2 else 0, chunks):
             relay_step(c, j)
     if last > 1:
         relay_step(0, last)

time: 29.4 us -> 31.2 us (1.061)
  Pallas kernels: 28.6 us -> 30.4 us
    pallas_call x1, Pallas kernels: 27.2 us -> 29 us  [fused(): pl.pallas_call(functools.partial(kernel, (zs, ss, rows, kvh, grp, hd)), o...]
where the time goes in v6:
time: 31.2 us; the launch traced here: 31.1 us
  Pallas kernels  30.4 us (97%)
  between operations  0.64 us (2%)
    pallas_call x1, Pallas kernels, fused(): pl.pallas_call(functools.partial(kernel, (zs, ss, rows, kvh, grp, hd)), o...  29 us
    pallas_call x1, Pallas kernels, written(): pl.pallas_call(tail_kernel, out_shape=tuple((jax.ShapeDtypeStruct(x.shape...  1.42 us

profile of v6, /device:TPU:0, one launch (start us, length us, event | category | flops | bytes accessed | tf_op | source)
XLA Modules:
  0.0 31.1 jit_solution(11618119604990508130)
XLA Ops:
  0.6 29.0 %span_grads.1 = (f32[128,32,128]{2,1,0:T(8,128)S(1)}, f32[256,128]{1,0:T(8,128)S(1)}, f32[256,128]{1,0:T(8,128)S(1)}) custom-call(s32[2,8]{1,0:T(2,128)} %bitcast.12, s32[1,128]{1,0:T(1,128)} %bitcast.13, f32[32,128]{1,0:T(8,128)} %bitcast.10, f32[32,128]{1,0:T(8,128)} %bitcast.11, bf16[256,128]{1,0:T(8,128)(2,1)} %bitcast.8, bf16[256,128]{1,0:T(8,128)(2,1)} %bitcast.9, ...), custom_call_target="tpu_custom_call" | custom-call | tf_op jit(solution)/shard_map/span_grads/pallas_call | solution.py:396
  29.6 1.4 %write_out.1 = (f32[128,32,128]{2,1,0:T(8,128)}, f32[256,128]{1,0:T(8,128)}, f32[256,128]{1,0:T(8,128)}) custom-call(f32[128,32,128]{2,1,0:T(8,128)S(1)} %get-tuple-element.9.dq_vm, f32[256,128]{1,0:T(8,128)S(1)} %get-tuple-element.10.dk_vm, f32[256,128]{1,0:T(8,128)S(1)} %get-tuple-element.11.dv_vm), custom_call_target="tpu_custom_call" | custom-call | tf_op jit(solution)/shard_map/write_out/pallas_call | solution.py:375
